TPU v7x, 512 devices: a whole 4x4x16 slice. The times are simulated.
512 devices in a mesh: dp: 32 (over y, z_lo), tensor: 16 (over x, z_hi, core).
Axes of the slice: x: 4, y: 4, z: 16 (z_hi: 2, z_lo: 8; z = z_hi * 8 + z_lo), core: 2. Of those that a mesh axis runs over, the one named last changes fastest.
Arguments:
- tokens: bfloat16 [16384, 4096], P(('dp', 'tensor')), may hold values from -6 to 6
- weight: bfloat16 [4096, 4096], P('tensor', 'dp'), may hold values from -0.09375 to 0.09375
Outputs:
- projected: bfloat16 [16384, 4096], P('dp', 'tensor')
All inputs are finite; a program needn't handle non-finite values.
Results may differ from a plain program's by a relative error of at most 0.0057.
Values may be sent and summed in bfloat16 or wider, within the bound.
A program may use at most 64 MiB of HBM per device.

v0:
```python
import jax
import jax.numpy as jnp
from jax import lax
from jax.sharding import PartitionSpec as P


def contract_last(left, right):
    return lax.dot_general(
        left, right, (((1,), (1,)), ((), ())), preferred_element_type=jnp.float32
    )


def contract_first(left, right):
    return lax.dot_general(
        left, right, (((0,), (0,)), ((), ())), preferred_element_type=jnp.float32
    )


def on_device(tokens, weight):
    col_slab = lax.all_gather(weight, "tensor", axis=0, tiled=True)
    term = contract_last(col_slab, weight)
    gram_cols = lax.psum(term, "dp").astype(jnp.bfloat16)
    update = 1.5 * weight.astype(jnp.float32) - 0.5 * contract_first(gram_cols, col_slab)
    ortho = update.astype(jnp.bfloat16)
    full_rows = lax.all_gather(ortho, "dp", axis=1, tiled=True)
    result = contract_last(lax.all_gather(tokens, "tensor", axis=0, tiled=True), full_rows)
    return result.astype(jnp.bfloat16)


def solution(mesh):
    placed = (P(("dp", "tensor"), None), P("tensor", "dp"))
    return jax.shard_map(
        on_device, mesh=mesh, in_specs=placed, out_specs=P("dp", "tensor"), check_vma=False
    )
```

profile of v0, /device:TPU:1, one launch (start us, length us, event | category | flops | bytes accessed | tf_op | source)
XLA Modules:
  0.0 695.2 jit_solution(15658774399451351064)
XLA Ops:
  6.5 0.0 all-gather.4.cloned.1.call-start
  6.5 0.7 all-gather.4.cloned.1.call-update
  7.3 0.0 all-gather.6.cloned.1.call-start
  7.3 86.7 %all-gather.4.cloned.1.call-done = bf16[4096,128]{1,0:T(8,128)(2,1)} async-done(((bf16[256,128]{1,0:T(8,128)(2,1)}), bf16[4096,128]{1,0:T(8,128)(2,1)}) %all-gather.4.cloned.1.call-update) | async-done | bytes 1048592 | tf_op jit(solution)/shard_map/all_gather | solution.py:20
  94.0 3.9 fusion.12
  97.9 0.0 copy-start
  97.9 0.0 copy-start.1
  97.9 255.6 %all-reduce.1 = bf16[4096,256]{1,0:T(8,128)(2,1)S(1)} all-reduce(f32[4096,256]{1,0:T(8,128)} %fusion.12), channel_id=1, replica_groups=mesh['dp'=32,'tensor'=16] {'dp'}, use_global_device_ids=true, to_apply=%region_0.0 | all-reduce | flops 1048576 | bytes 6291456 | tf_op jit(solution)/shard_map/psum | solution.py:22
  353.5 0.0 copy-done
  353.5 0.0 copy-done.1
  353.5 1.4 fusion.9
  354.9 0.0 all-gather.6.cloned.1.call-update
  354.9 0.0 all-gather.8.cloned.1.call-start
  354.9 0.7 all-gather.8.cloned.1.call-update
  355.6 193.9 %all-gather.6.cloned.1.call-done = bf16[256,4096]{1,0:T(8,128)(2,1)} async-done(((bf16[256,128]{1,0:T(8,128)(2,1)}), bf16[256,4096]{1,0:T(8,128)(2,1)}) %all-gather.6.cloned.1.call-update) | async-done | bytes 2097168 | tf_op jit(solution)/shard_map/all_gather | solution.py:25
  549.5 134.2 %all-gather.8.cloned.1.call-done = bf16[512,4096]{1,0:T(8,128)(2,1)} async-done(((bf16[32,4096]{1,0:T(8,128)(2,1)}), bf16[512,4096]{1,0:T(8,128)(2,1)}) %all-gather.8.cloned.1.call-update) | async-done | bytes 4194320 | tf_op jit(solution)/shard_map/all_gather | solution.py:26
  683.7 4.1 fusion.2
  687.9 0.8 copy.3
Async XLA Ops:
  6.5 87.5 %all-gather.4.cloned.1.call-start = ((), (), s32[]{:S(2)}) async-start(), calls=%async_computation | async-start | bytes 1114112 | tf_op jit(solution)/shard_map/all_gather | solution.py:20
  7.3 542.3 %all-gather.6.cloned.1.call-start = ((), (), s32[]{:S(2)}) async-start(), calls=%async_computation.1 | async-start | bytes 2162688 | tf_op jit(solution)/shard_map/all_gather | solution.py:25
  97.9 255.6 %copy-start = (bf16[4096,128]{1,0:T(8,128)(2,1)S(1)}, bf16[4096,128]{1,0:T(8,128)(2,1)}, u32[]{:S(2)}) copy-start(bf16[4096,128]{1,0:T(8,128)(2,1)} %all-gather.4.cloned.1.call-done) | copy-start | bytes 3145732
  97.9 255.6 %copy-start.1 = (bf16[256,128]{1,0:T(8,128)(2,1)S(1)}, bf16[256,128]{1,0:T(8,128)(2,1)}, u32[]{:S(2)}) copy-start(bf16[256,128]{1,0:T(8,128)(2,1)} %param.3) | copy-start | bytes 196612
  354.9 328.9 %all-gather.8.cloned.1.call-start = ((), (), s32[]{:S(2)}) async-start(), calls=%async_computation.2 | async-start | bytes 4456448 | tf_op jit(solution)/shard_map/all_gather | solution.py:26
Sparse Core Ops, SparseCore 0:
  10.6 83.3 all-gather.3
  355.0 194.4 all-gather.5
  552.8 130.8 all-gather.7
where the time goes:
time: 695 us
  waiting for transfers between devices  416 us (60%)
  blocking collectives  256 us (37%)
  between operations  13.1 us (2%)
  matrix products  9.36 us (1%)
    psum x1, blocking collectives, on_device(): gram_cols = lax.psum(term, 'dp').astype(jnp.bfloat16)  256 us
    all_gather x1, waiting for transfers between devices, on_device(): full_rows = lax.all_gather(ortho, 'dp', axis=1, tiled=True)  194 us
    all_gather x1, waiting for transfers between devices, on_device(): lax.all_gather(tokens, 'tensor', axis=0, tiled=True)  134 us
    all_gather x1, waiting for transfers between devices, on_device(): col_slab = lax.all_gather(weight, 'tensor', axis=0, tiled=True)  86.7 us
  transfers between devices with their start and end apart: 3, of which 3 were waited for; matrix products, arithmetic and copies ran while one was open for 0% of the time, Pallas kernels for 0%

commit v1 on v0

--- a/solution.py
+++ b/solution.py
@@ -23,7 +23,12 @@
     update = 1.5 * weight.astype(jnp.float32) - 0.5 * contract_first(gram_cols, col_slab)
     ortho = update.astype(jnp.bfloat16)
     full_rows = lax.all_gather(ortho, "dp", axis=1, tiled=True)
-    result = contract_last(lax.all_gather(tokens, "tensor", axis=0, tiled=True), full_rows)
+    result = contract_last(
+        jnp.concatenate(
+            lax.all_to_all(jnp.stack([tokens] * lax.axis_size("tensor")), "tensor", 0, 0), axis=0
+        ),
+        full_rows,
+    )
     return result.astype(jnp.bfloat16)
 
 

time: 695 us -> 735 us (1.058)
  the two profiles are of different devices: /device:TPU:1 before, /device:TPU:2 now
where the time goes in v1:
time: 735 us
  waiting for transfers between devices  380 us (52%)
  blocking collectives  310 us (42%)
  starting transfers between devices  18.3 us (2%)
  between operations  13.4 us (2%)
  matrix products  9.39 us (1%)
    psum x1, blocking collectives, on_device(): gram_cols = lax.psum(term, 'dp').astype(jnp.bfloat16)  310 us
    all_gather x1, waiting for transfers between devices, on_device(): full_rows = lax.all_gather(ortho, 'dp', axis=1, tiled=True)  191 us
    all_gather x1, waiting for transfers between devices, on_device(): col_slab = lax.all_gather(weight, 'tensor', axis=0, tiled=True)  188 us
    all_to_all x1, starting transfers between devices, on_device(): lax.all_to_all(jnp.stack([tokens] * lax.axis_size('tensor')), 'tensor', 0...  18.2 us
  transfers between devices with their start and end apart: 3, of which 2 were waited for; matrix products, arithmetic and copies ran while one was open for 1% of the time, Pallas kernels for 0%

profile of v1, /device:TPU:2, one launch (start us, length us, event | category | flops | bytes accessed | tf_op | source)
XLA Modules:
  0.0 734.6 jit_solution(15140792650123389097)
XLA Ops:
  6.5 3.4 stack.2
  10.0 0.0 copy-start.1
  10.0 18.2 %all-to-all-start = ((bf16[16,32,4096]{2,1,0:T(8,128)(2,1)}), bf16[16,32,4096]{2,1,0:T(8,128)(2,1)}, u32[]{:S(2)}, u32[]{:S(2)}) async-start(bf16[16,32,4096]{2,1,0:T(8,128)(2,1)} %stack.2), calls=%async_computation | async-start | bytes 8388608 | tf_op jit(solution)/shard_map/all_to_all | solution.py:28
  28.2 0.0 all-gather.3.cloned.1.call-start
  28.3 0.7 all-gather.3.cloned.1.call-update
  28.9 0.0 all-gather.5.cloned.1.call-start
  29.0 188.3 %all-gather.3.cloned.1.call-done = bf16[4096,128]{1,0:T(8,128)(2,1)} async-done(((bf16[256,128]{1,0:T(8,128)(2,1)}), bf16[4096,128]{1,0:T(8,128)(2,1)}) %all-gather.3.cloned.1.call-update) | async-done | bytes 1048592 | tf_op jit(solution)/shard_map/all_gather | solution.py:20
  217.3 0.0 copy-done.1
  217.3 3.9 fusion.12
  221.2 0.0 copy-start
  221.2 309.7 %all-reduce.1 = bf16[4096,256]{1,0:T(8,128)(2,1)S(1)} all-reduce(f32[4096,256]{1,0:T(8,128)} %fusion.12), channel_id=1, replica_groups=mesh['dp'=32,'tensor'=16] {'dp'}, use_global_device_ids=true, to_apply=%region_0.0 | all-reduce | flops 1048576 | bytes 6291456 | tf_op jit(solution)/shard_map/psum | solution.py:22
  530.9 0.0 copy-done
  530.9 1.4 fusion.9
  532.3 0.0 all-gather.5.cloned.1.call-update
  532.3 190.5 %all-gather.5.cloned.1.call-done = bf16[256,4096]{1,0:T(8,128)(2,1)} async-done(((bf16[256,128]{1,0:T(8,128)(2,1)}), bf16[256,4096]{1,0:T(8,128)(2,1)}) %all-gather.5.cloned.1.call-update) | async-done | bytes 2097168 | tf_op jit(solution)/shard_map/all_gather | solution.py:25
  722.8 0.0 all-to-all-done
  722.8 4.1 fusion.2
  726.9 0.8 copy.3
Async XLA Ops:
  10.0 207.3 %copy-start.1 = (bf16[256,128]{1,0:T(8,128)(2,1)S(1)}, bf16[256,128]{1,0:T(8,128)(2,1)}, u32[]{:S(2)}) copy-start(bf16[256,128]{1,0:T(8,128)(2,1)} %param.3) | copy-start | bytes 196612
  10.0 712.8 %all-to-all-start = ((bf16[16,32,4096]{2,1,0:T(8,128)(2,1)}), bf16[16,32,4096]{2,1,0:T(8,128)(2,1)}, u32[]{:S(2)}, u32[]{:S(2)}) async-start(bf16[16,32,4096]{2,1,0:T(8,128)(2,1)} %stack.2), calls=%async_computation | async-start | bytes 8388608 | tf_op jit(solution)/shard_map/all_to_all | solution.py:28
  28.2 189.1 %all-gather.3.cloned.1.call-start = ((), (), s32[]{:S(2)}) async-start(), calls=%async_computation.1 | async-start | bytes 1114112 | tf_op jit(solution)/shard_map/all_gather | solution.py:20
  28.9 693.9 %all-gather.5.cloned.1.call-start = ((), (), s32[]{:S(2)}) async-start(), calls=%async_computation.2 | async-start | bytes 2162688 | tf_op jit(solution)/shard_map/all_gather | solution.py:25
  221.2 309.7 %copy-start = (bf16[4096,128]{1,0:T(8,128)(2,1)S(1)}, bf16[4096,128]{1,0:T(8,128)(2,1)}, u32[]{:S(2)}) copy-start(bf16[4096,128]{1,0:T(8,128)(2,1)} %all-gather.3.cloned.1.call-done) | copy-start | bytes 3145732
Sparse Core Ops, SparseCore 0:
  32.3 184.9 all-gather.2
  532.4 190.3 all-gather.4
